TPU v7x, 32 devices: a whole 2x2x4 slice. The times are simulated.
32 devices in a mesh: row: 8 (over z, core), col: 4 (over y, x).
Axes of the slice: x: 2, y: 2, z: 4, core: 2. Of those that a mesh axis runs over, the one named last changes fastest.
Arguments:
- start_block: bfloat16 [16, 4096], P(None, 'col'), may hold values from -33 to 33
- block_values: bfloat16 [8, 4, 12, 128, 128], P('row', 'col'), may hold values from -0.109375 to 0.109375
- block_columns: int32 [8, 4, 12], P('row', 'col'), may hold values from 0 to 7
- block_counts: int32 [8, 4, 4], P('row', 'col'), may hold values from 1 to 6, 12 in all within a row
Outputs:
- applied_once: bfloat16 [16, 4096], P(None, 'row')
- applied_twice: bfloat16 [16, 4096], P(None, 'row')
- basis_gram: float32 [32, 32], replicated
- projected_gram: float32 [32, 32], replicated
All inputs are finite; a program needn't handle non-finite values.
Results may differ from a plain program's by a relative error of at most 0.0039.
Values may be sent and summed in bfloat16 or wider, within the bound.
No kernel may reach another device: no remote copies, remote signals or barrier semaphores. Data moves between devices by JAX's collectives and lax.ppermute only.
A program may use at most 64 MiB of HBM per device.

v0:
```python
import jax
import jax.numpy as jnp
from jax import lax
from jax.sharding import PartitionSpec as P

highest = lax.Precision.HIGHEST


def broadcast(block, axis, owner):
    block = jnp.where(lax.axis_index(axis) == owner, block, jnp.zeros_like(block))
    return lax.psum(block, axis)


def block_rows_of(counts, block_total):
    row_ends = jnp.cumsum(counts)
    positions = jnp.arange(block_total, dtype=jnp.int32)
    return jnp.sum((row_ends[None, :] <= positions[:, None]).astype(jnp.int32), axis=1)


def forward_tile(values, columns, block_row, source, row_blocks):
    vector_count = source.shape[0]
    block_size = values.shape[1]
    pieces = source.reshape(vector_count, -1, block_size)[:, columns, :]
    products = jnp.einsum("bij,kbj->kbi", values, pieces, preferred_element_type=jnp.float32)
    row_hot = (block_row[:, None] == jnp.arange(row_blocks, dtype=jnp.int32)[None, :]).astype(
        jnp.float32
    )
    summed = jnp.einsum("kbi,br->kri", products, row_hot, precision=highest)
    return summed.reshape(vector_count, row_blocks * block_size)


def transpose_tile(values, columns, block_row, source, col_blocks):
    vector_count = source.shape[0]
    block_size = values.shape[1]
    pieces = source.reshape(vector_count, -1, block_size)[:, block_row, :]
    products = jnp.einsum("bji,kbj->kbi", values, pieces, preferred_element_type=jnp.float32)
    col_hot = (columns[:, None] == jnp.arange(col_blocks, dtype=jnp.int32)[None, :]).astype(
        jnp.float32
    )
    summed = jnp.einsum("kbi,bc->kci", products, col_hot, precision=highest)
    return summed.reshape(vector_count, col_blocks * block_size)


def inner_products(left_block, right_block):
    return jnp.dot(left_block, right_block.T, precision=highest)


def local(start_block, block_values, block_columns, block_counts):
    values = block_values[0, 0]
    columns = block_columns[0, 0]
    counts = block_counts[0, 0]
    block_size = values.shape[1]
    row_blocks = counts.shape[0]
    row_width = row_blocks * block_size
    col_width = start_block.shape[1]
    col_blocks = col_width // block_size
    block_row = block_rows_of(counts, values.shape[0])
    row_slot = lax.axis_index("row")
    col_slot = lax.axis_index("col")
    slab_ratio = lax.axis_size("row") // lax.axis_size("col")
    owner_col = row_slot // slab_ratio
    offset = row_slot % slab_ratio * row_width
    on_owner = col_slot == owner_col
    piece_len = row_width // lax.axis_size("col")
    norm_scale = 1.0 / (row_width * lax.axis_size("row"))

    def piece_of(vectors):
        return lax.dynamic_slice_in_dim(vectors, col_slot * piece_len, piece_len, 1)

    def apply_operator(col_part, row_part):
        forward = forward_tile(values, columns, block_row, col_part, row_blocks)
        backward = transpose_tile(values, columns, block_row, row_part, col_blocks)
        column_total = lax.psum(backward, "row")
        owner_share = lax.dynamic_slice_in_dim(column_total, offset, row_width, 1)
        row_term = forward + jnp.where(on_owner, owner_share, 0.0)
        whole_slab = lax.psum(row_term, "col").astype(jnp.bfloat16)
        own_piece = piece_of(whole_slab)
        return (whole_slab, own_piece.astype(jnp.float32))

    root_slab = broadcast(start_block, "col", owner_col)
    start_rows = lax.dynamic_slice_in_dim(root_slab, offset, row_width, 1)
    applied_once, once_piece = apply_operator(start_block, start_rows)
    start_piece = piece_of(start_rows).astype(jnp.float32)
    slab_parts = []
    for turn_index in range(slab_ratio):
        slab_parts.append(broadcast(applied_once, "row", col_slot * slab_ratio + turn_index))
    once_columns = jnp.concatenate(slab_parts, axis=1)
    applied_twice, twice_piece = apply_operator(once_columns, applied_once)
    gram_xx, gram_xy, gram_yy, gram_yz = lax.psum(
        (
            inner_products(start_piece, start_piece),
            inner_products(start_piece, once_piece),
            inner_products(once_piece, once_piece),
            inner_products(once_piece, twice_piece),
        ),
        ("row", "col"),
    )
    basis_gram = (
        jnp.concatenate(
            [jnp.concatenate([gram_xx, gram_xy], 1), jnp.concatenate([gram_xy.T, gram_yy], 1)], 0
        )
        * norm_scale
    )
    projected_gram = (
        jnp.concatenate(
            [jnp.concatenate([gram_xy, gram_yy], 1), jnp.concatenate([gram_yy, gram_yz], 1)], 0
        )
        * norm_scale
    )
    return (applied_once, applied_twice, basis_gram, projected_gram)


def solution(mesh):
    return jax.shard_map(
        local,
        mesh=mesh,
        in_specs=(
            P(None, "col"),
            P("row", "col", None, None, None),
            P("row", "col", None),
            P("row", "col", None),
        ),
        out_specs=(P(None, "row"), P(None, "row"), P(), P()),
        check_vma=False,
    )
```

profile of v0, /device:TPU:0, one launch (start us, length us, event | category | flops | bytes accessed | tf_op | source)
XLA Modules:
  0.0 240.9 jit_solution(7945162154595536846)
XLA Ops:
  7.2 0.0 copy-start
  7.2 0.0 copy-start.2
  7.2 0.0 all-reduce.5.cloned.1.call-start
  7.2 0.8 reduce-window.8
  8.1 0.1 convert_reduce_fusion
  8.2 0.0 copy-done.2
  8.2 17.8 %psum.77 = bf16[16,1024]{1,0:T(8,128)(2,1)S(1)} all-reduce(bf16[16,1024]{1,0:T(8,128)(2,1)S(1)} %broadcast_select_fusion), channel_id=1, replica_groups=mesh['row'=8,'col'=4] {'col'}, use_global_device_ids=true, to_apply=%region_2.3 | all-reduce | flops 16384 | bytes 65536 | tf_op jit(solution)/shard_map/psum | solution.py:11
  26.0 0.6 gather_fusion.1
  26.6 0.0 copy-done
  26.6 0.2 convolution_bitcast_fusion.2
  26.8 0.0 copy-start.4
  26.8 0.7 copy-done.4
  27.5 0.2 fusion.8
  27.6 0.6 copy.57
  28.3 0.0 all-reduce.5.cloned.1.call-update
  28.3 0.0 all-reduce.7.cloned.1.call-start
  28.4 0.6 gather_fusion
  29.0 0.3 convolution_bitcast_fusion.3
  29.3 0.2 fusion.10
  29.5 0.2 fusion.23
  29.7 51.8 %all-reduce.5.cloned.1.call-done = f32[16,1024]{1,0:T(8,128)} async-done(((f32[16,1024]{1,0:T(8,128)}), f32[16,1024]{1,0:T(8,128)}) %all-reduce.5.cloned.1.call-update) | async-done | bytes 65552 | tf_op jit(solution)/shard_map/psum | solution.py:73
  81.4 0.8 bitcast_add_fusion.1
  82.2 16.2 %psum.79 = bf16[16,512]{1,0:T(8,128)(2,1)S(1)} all-reduce(f32[16,512]{1,0:T(8,128)S(1)} %bitcast_add_fusion.1), channel_id=1, replica_groups=mesh['row'=8,'col'=4] {'col'}, use_global_device_ids=true, to_apply=%region_4.5 | all-reduce | flops 8192 | bytes 49152 | tf_op jit(solution)/shard_map/psum | solution.py:76
  98.4 0.0 copy-start.1
  98.5 0.1 fusion.26
  98.6 26.0 %all-reduce.1 = (bf16[16,512]{1,0:T(8,128)(2,1)S(1)}, bf16[16,512]{1,0:T(8,128)(2,1)S(1)}) all-reduce(bf16[16,512]{1,0:T(8,128)(2,1)S(1)} %get-tuple-element.11, bf16[16,512]{1,0:T(8,128)(2,1)S(1)} %get-tuple-element.10), channel_id=1, replica_groups=mesh['row'=8,'col'=4] {'row'}, use_global_device_ids=true, to_apply=%region_6.7 | all-reduce | flops 16384 | bytes 65536 | tf_op jit(solution)/shard_map/psum | solution.py:11
  124.6 0.6 gather_fusion.2
  125.2 0.3 convolution_bitcast_fusion.1
  125.5 0.2 fusion.6
  125.7 0.6 gather_fusion.3
  126.2 0.2 convolution_bitcast_fusion
  126.4 0.2 fusion.4
  126.6 0.6 copy.56
  127.3 0.0 all-reduce.7.cloned.1.call-update
  127.3 0.2 fusion.21
  127.5 49.9 %all-reduce.7.cloned.1.call-done = f32[16,1024]{1,0:T(8,128)} async-done(((f32[16,1024]{1,0:T(8,128)}), f32[16,1024]{1,0:T(8,128)}) %all-reduce.7.cloned.1.call-update) | async-done | bytes 65552 | tf_op jit(solution)/shard_map/psum | solution.py:73
  177.4 0.8 bitcast_add_fusion
  178.2 16.2 %psum.83 = bf16[16,512]{1,0:T(8,128)(2,1)S(1)} all-reduce(f32[16,512]{1,0:T(8,128)S(1)} %bitcast_add_fusion), channel_id=1, replica_groups=mesh['row'=8,'col'=4] {'col'}, use_global_device_ids=true, to_apply=%region_8.9 | all-reduce | flops 8192 | bytes 49152 | tf_op jit(solution)/shard_map/psum | solution.py:76
  194.4 0.0 copy-done.1
  194.4 0.0 copy-start.3
  194.4 0.1 fusion.16
  194.5 38.7 %all-reduce = (f32[16,16]{1,0:T(8,128)S(1)}, f32[16,16]{1,0:T(8,128)S(1)}, f32[16,16]{1,0:T(8,128)S(1)}, f32[16,16]{1,0:T(8,128)S(1)}) all-reduce(f32[16,16]{1,0:T(8,128)S(1)} %fusion.26, f32[16,16]{1,0:T(8,128)S(1)} %fusion.21, f32[16,16]{1,0:T(8,128)S(1)} %fusion.23, ...), channel_id=1, replica_groups=mesh['row'=8,'col'=4] {'row','col'}, use_global_device_ids=true, to_apply=%region_11.12 | all-reduce | flops 1024 | bytes 8192 | tf_op jit(solution)/shard_map/psum | solution.py:89
  233.2 0.0 copy-done.3
  233.2 0.1 copy.30
  233.3 0.1 copy.31
  233.4 0.7 maximum_multiply_fusion.1
  (11 shorter events, 0.1 us)
Async XLA Ops:
  7.2 19.4 %copy-start = (bf16[1,1,12,128,128]{4,3,2,1,0:T(8,128)(2,1)S(1)}, bf16[1,1,12,128,128]{4,3,2,1,0:T(8,128)(2,1)}, u32[]{:S(2)}) copy-start(bf16[1,1,12,128,128]{4,3,2,1,0:T(8,128)(2,1)} %param.5) | copy-start | bytes 1179652
  7.2 1.0 copy-start.2
  7.2 74.3 %all-reduce.5.cloned.1.call-start = ((), (), s32[]{:S(2)}) async-start(), calls=%async_computation | async-start | bytes 131072 | tf_op jit(solution)/shard_map/psum | solution.py:73
  26.8 0.7 copy-start.4
  28.3 149.1 %all-reduce.7.cloned.1.call-start = ((), (), s32[]{:S(2)}) async-start(), calls=%async_computation.1 | async-start | bytes 131072 | tf_op jit(solution)/shard_map/psum | solution.py:73
  98.4 95.9 %copy-start.1 = (bf16[16,512]{1,0:T(8,128)(2,1)}, bf16[16,512]{1,0:T(8,128)(2,1)S(1)}, u32[]{:S(2)}) copy-start(bf16[16,512]{1,0:T(8,128)(2,1)S(1)} %psum.79) | copy-start | bytes 49156
  194.4 38.8 %copy-start.3 = (bf16[16,512]{1,0:T(8,128)(2,1)}, bf16[16,512]{1,0:T(8,128)(2,1)S(1)}, u32[]{:S(2)}) copy-start(bf16[16,512]{1,0:T(8,128)(2,1)S(1)} %psum.83) | copy-start | bytes 49156
Sparse Core Ops, SparseCore 0:
  28.4 52.9 all-reduce.4
  127.4 49.9 all-reduce.6
where the time goes:
time: 241 us
  blocking collectives  115 us (48%)
  waiting for transfers between devices  102 us (42%)
  between operations  14.3 us (6%)
  local copies, waits for them, and re-layouts  4.37 us (2%)
  other arithmetic  3.19 us (1%)
  matrix products  2.45 us (1%)
    psum x2, waiting for transfers between devices, apply_operator(): column_total = lax.psum(backward, 'row')  102 us
    psum x2, blocking collectives, broadcast(): return lax.psum(block, axis)  43.7 us
    psum x1, blocking collectives, local(): lax.psum((inner_products(start_piece, start_piece), inner_products(start_...  38.7 us
    psum x2, blocking collectives, apply_operator(): whole_slab = lax.psum(row_term, 'col').astype(jnp.bfloat16)  32.5 us
  transfers between devices with their start and end apart: 2, of which 2 were waited for; matrix products, arithmetic and copies ran while one was open for 1% of the time, Pallas kernels for 0%

commit v1 on v0

--- a/solution.py
+++ b/solution.py
@@ -70,7 +70,7 @@
     def apply_operator(col_part, row_part):
         forward = forward_tile(values, columns, block_row, col_part, row_blocks)
         backward = transpose_tile(values, columns, block_row, row_part, col_blocks)
-        column_total = lax.psum(backward, "row")
+        column_total = jnp.sum(lax.all_gather(backward, "row"), axis=0)
         owner_share = lax.dynamic_slice_in_dim(column_total, offset, row_width, 1)
         row_term = forward + jnp.where(on_owner, owner_share, 0.0)
         whole_slab = lax.psum(row_term, "col").astype(jnp.bfloat16)

time: 241 us -> 154 us (0.64)
  waiting for transfers between devices: 102 us -> 0 us
  blocking collectives: 115 us -> 144 us
  between operations: 14.3 us -> 0.86 us
    psum x2 -> x0, waiting for transfers between devices: 102 us -> none  [apply_operator(): column_total = lax.psum(backward, 'row')]
    all_gather x0 -> x2, blocking collectives: none -> 30.4 us  [apply_operator(): column_total = jnp.sum(lax.all_gather(backward, 'row'), axis=0)]
    psum x2, blocking collectives: 43.7 us -> 46.6 us  [broadcast(): return lax.psum(block, axis)]
    psum x2, blocking collectives: 32.5 us -> 29.8 us  [apply_operator(): whole_slab = lax.psum(row_term, 'col').astype(jnp.bfloat16)]
  transfers between devices with their start and end apart: 2 -> 0, of which waited for: 2 -> 0; matrix products, arithmetic and copies ran while one was open for 1% -> 0% of each run, Pallas kernels for 0% -> 0%
where the time goes in v1:
time: 154 us; the launch traced here: 153 us
  blocking collectives  144 us (94%)
  local copies, waits for them, and re-layouts  4.84 us (3%)
  matrix products  2.42 us (2%)
    psum x2, blocking collectives, broadcast(): return lax.psum(block, axis)  46.6 us
    psum x1, blocking collectives, local(): lax.psum((inner_products(start_piece, start_piece), inner_products(start_...  37.2 us
    all_gather x2, blocking collectives, apply_operator(): column_total = jnp.sum(lax.all_gather(backward, 'row'), axis=0)  30.4 us
    psum x2, blocking collectives, apply_operator(): whole_slab = lax.psum(row_term, 'col').astype(jnp.bfloat16)  29.8 us

profile of v1, /device:TPU:0, one launch (start us, length us, event | category | flops | bytes accessed | tf_op | source)
XLA Modules:
  0.0 153.3 jit_solution(17650192492687448171)
XLA Ops:
  0.6 0.0 copy-start
  0.6 0.0 copy-start.2
  0.7 0.8 copy-done.2
  1.5 17.7 %psum.63 = bf16[16,1024]{1,0:T(8,128)(2,1)S(1)} all-reduce(bf16[16,1024]{1,0:T(8,128)(2,1)S(1)} %broadcast_select_fusion), channel_id=1, replica_groups=mesh['row'=8,'col'=4] {'col'}, use_global_device_ids=true, to_apply=%region_2.3 | all-reduce | flops 16384 | bytes 65536 | tf_op jit(solution)/shard_map/psum | solution.py:11
  19.2 0.0 copy-start.5
  19.2 0.6 copy-done.5
  19.9 0.2 reduce-window.8
  20.1 0.1 convert_reduce_fusion
  20.2 0.6 gather_fusion.1
  20.7 0.0 copy-done
  20.7 0.2 convolution_bitcast_fusion.2
  21.0 0.0 copy-start.4
  21.0 0.7 copy-done.4
  21.6 0.2 convolution_bitcast_fusion.5
  21.8 15.4 %all_gather.6 = f32[8,16,1024]{2,1,0:T(8,128)S(1)} all-gather(f32[1,16,1024]{2,1,0:T(8,128)S(1)} %all_gather_reshape.6), channel_id=1, replica_groups=mesh['row'=8,'col'=4] {'row'}, dimensions={0}, use_global_device_ids=true | all-gather | bytes 589824 | tf_op jit(solution)/shard_map/all_gather | solution.py:73
  37.3 0.6 gather_fusion
  37.9 0.3 convolution_bitcast_fusion.3
  38.2 0.2 fusion.8
  38.4 14.3 %psum.64 = bf16[16,512]{1,0:T(8,128)(2,1)S(1)} all-reduce(f32[16,512]{1,0:T(8,128)S(1)} %bitcast_add_fusion.1), channel_id=1, replica_groups=mesh['row'=8,'col'=4] {'col'}, use_global_device_ids=true, to_apply=%region_4.5 | all-reduce | flops 8192 | bytes 49152 | tf_op jit(solution)/shard_map/psum | solution.py:76
  52.8 0.0 copy-start.1
  52.8 0.6 gather_fusion.3
  53.3 0.2 convolution_bitcast_fusion
  53.6 0.2 convolution_bitcast_fusion.4
  53.8 15.0 %all_gather.7 = f32[8,16,1024]{2,1,0:T(8,128)S(1)} all-gather(f32[1,16,1024]{2,1,0:T(8,128)S(1)} %all_gather_reshape.7), channel_id=1, replica_groups=mesh['row'=8,'col'=4] {'row'}, dimensions={0}, use_global_device_ids=true | all-gather | bytes 589824 | tf_op jit(solution)/shard_map/all_gather | solution.py:73
  68.9 28.8 %all-reduce.1 = (bf16[16,512]{1,0:T(8,128)(2,1)S(1)}, bf16[16,512]{1,0:T(8,128)(2,1)S(1)}) all-reduce(bf16[16,512]{1,0:T(8,128)(2,1)S(1)} %get-tuple-element.11, bf16[16,512]{1,0:T(8,128)(2,1)S(1)} %get-tuple-element.10), channel_id=1, replica_groups=mesh['row'=8,'col'=4] {'row'}, use_global_device_ids=true, to_apply=%region_6.7 | all-reduce | flops 16384 | bytes 65536 | tf_op jit(solution)/shard_map/psum | solution.py:11
  97.7 0.6 gather_fusion.2
  98.3 0.3 convolution_bitcast_fusion.1
  98.6 0.2 fusion.5
  98.8 15.5 %psum.67 = bf16[16,512]{1,0:T(8,128)(2,1)S(1)} all-reduce(f32[16,512]{1,0:T(8,128)S(1)} %bitcast_add_fusion), channel_id=1, replica_groups=mesh['row'=8,'col'=4] {'col'}, use_global_device_ids=true, to_apply=%region_8.9 | all-reduce | flops 8192 | bytes 49152 | tf_op jit(solution)/shard_map/psum | solution.py:76
  114.3 0.0 copy-start.3
  114.3 0.1 fusion.14
  114.4 0.2 fusion.19
  114.6 0.0 copy-done.1
  114.6 0.3 copy-done.3
  114.9 0.1 fusion.24
  115.0 0.2 fusion.21
  115.2 37.2 %all-reduce = (f32[16,16]{1,0:T(8,128)S(1)}, f32[16,16]{1,0:T(8,128)S(1)}, f32[16,16]{1,0:T(8,128)S(1)}, f32[16,16]{1,0:T(8,128)S(1)}) all-reduce(f32[16,16]{1,0:T(8,128)S(1)} %fusion.24, f32[16,16]{1,0:T(8,128)S(1)} %fusion.19, f32[16,16]{1,0:T(8,128)S(1)} %fusion.21, ...), channel_id=1, replica_groups=mesh['row'=8,'col'=4] {'row','col'}, use_global_device_ids=true, to_apply=%region_11.12 | all-reduce | flops 1024 | bytes 8192 | tf_op jit(solution)/shard_map/psum | solution.py:89
  152.5 0.1 copy.40
  152.5 0.1 copy.41
  152.6 0.7 maximum_multiply_fusion.1
  (17 shorter events, 0.2 us)
Async XLA Ops:
  0.6 20.1 %copy-start = (bf16[1,1,12,128,128]{4,3,2,1,0:T(8,128)(2,1)S(1)}, bf16[1,1,12,128,128]{4,3,2,1,0:T(8,128)(2,1)}, u32[]{:S(2)}) copy-start(bf16[1,1,12,128,128]{4,3,2,1,0:T(8,128)(2,1)} %param.5) | copy-start | bytes 1179652
  0.6 0.8 copy-start.2
  19.2 0.7 copy-start.5
  21.0 0.7 copy-start.4
  52.8 61.9 %copy-start.1 = (bf16[16,512]{1,0:T(8,128)(2,1)}, bf16[16,512]{1,0:T(8,128)(2,1)S(1)}, u32[]{:S(2)}) copy-start(bf16[16,512]{1,0:T(8,128)(2,1)S(1)} %psum.64) | copy-start | bytes 49156
  114.3 0.6 copy-start.3
